TPU v7x, 32 devices: a whole 2x2x4 slice. The times are simulated.
32 devices in a mesh: row: 8 (over y, x, core), col: 4 (over z).
Axes of the slice: x: 2, y: 2, z: 4, core: 2. Of those that a mesh axis runs over, the one named last changes fastest.
Arguments:
- descriptors: bfloat16 [32, 6144], P(None, ('row', 'col')), may hold values from -6 to 6
- densities: float32 [6144], P(('row', 'col')), may hold values from 0.25 to 4
- vectors: float32 [32, 6144], P(None, ('row', 'col')), may hold values from -6 to 6
Outputs:
- next_block: float32 [32, 6144], P(None, ('row', 'col'))
All inputs are finite; a program needn't handle non-finite values.
Results may differ from a plain program's by a relative error of at most 0.0036.
Values may be sent and summed in bfloat16 or wider, within the bound.
No kernel may reach another device: no remote copies, remote signals or barrier semaphores. Data moves between devices by JAX's collectives and lax.ppermute only.
A program may use at most 64 MiB of HBM per device.

v0:
```python
import math

import jax
import jax.numpy as jnp
from jax import lax
from jax.sharding import PartitionSpec as P

kernel_width = 8.0


def tile_terms(targets, target_norm, piece):
    piece_feat, piece_vals, piece_inv = piece
    piece_norm = jnp.sum(jnp.square(piece_feat.astype(jnp.float32)), axis=0)
    feature_dim, target_count = targets.shape
    span_rows = math.gcd(target_count, 512)
    block_count = target_count // span_rows
    blocks = targets.reshape(feature_dim, block_count, span_rows).transpose(1, 0, 2)
    norm_blocks = target_norm.reshape(block_count, span_rows)

    def tile_block(block_item):
        block_feat, block_norm = block_item
        inner_prod = lax.dot_general(
            block_feat, piece_feat, (((0,), (0,)), ((), ())), preferred_element_type=jnp.float32
        )
        kernel = jnp.exp(
            -(block_norm[:, None] + piece_norm[None, :] - 2.0 * inner_prod) / kernel_width
        ).astype(jnp.bfloat16)
        numerator = lax.dot_general(
            piece_vals, kernel, (((1,), (1,)), ((), ())), preferred_element_type=jnp.float32
        )
        degree = lax.dot_general(
            piece_inv, kernel, (((1,), (1,)), ((), ())), preferred_element_type=jnp.float32
        )
        return (numerator, degree)

    numerator, degree = lax.map(tile_block, (blocks, norm_blocks))
    numerator = numerator.transpose(1, 0, 2).reshape(piece_vals.shape[0], target_count)
    degree = degree.transpose(1, 0, 2).reshape(1, target_count)
    return (numerator, degree)


def accumulate(targets, vec_count):
    target_norm = jnp.sum(jnp.square(targets.astype(jnp.float32)), axis=0)

    def fold_piece(running, piece, start):
        numerator, degree = tile_terms(targets, target_norm, piece)
        return (numerator, degree)

    initial = (
        jnp.zeros((vec_count, targets.shape[1]), jnp.float32),
        jnp.zeros((1, targets.shape[1]), jnp.float32),
    )
    return (fold_piece, initial)


def per_device(descriptors, densities, vectors):
    highest = lax.Precision.HIGHEST
    vec_count = vectors.shape[0]
    weighted = (vectors / densities[None, :]).astype(jnp.bfloat16)
    inverse = (1.0 / densities).astype(jnp.bfloat16)[None, :]
    targets = lax.all_gather(descriptors, "col", axis=1, tiled=True)
    fold_piece, initial = accumulate(targets, vec_count)
    partial_value = fold_piece(
        initial,
        (
            lax.all_gather(descriptors, "row", axis=1, tiled=True),
            lax.all_gather(weighted, "row", axis=1, tiled=True),
            lax.all_gather(inverse, "row", axis=1, tiled=True),
        ),
        jnp.int32(0),
    )
    numerator, degree = (
        lax.psum_scatter(partial_value[0], "col", scatter_dimension=1, tiled=True),
        lax.psum_scatter(partial_value[1], "col", scatter_dimension=1, tiled=True),
    )
    diffused = numerator / degree
    samples_float = float(descriptors.shape[1] * lax.axis_size("row") * lax.axis_size("col"))
    coupling, diffused_gram, basis_gram = lax.psum(
        (
            jnp.dot(vectors, diffused.T, precision=highest),
            jnp.dot(diffused, diffused.T, precision=highest),
            jnp.dot(vectors, vectors.T, precision=highest),
        ),
        ("row", "col"),
    )
    remainder = diffused - jnp.dot(coupling.T, vectors, precision=highest) / samples_float
    cross_term = jnp.dot(coupling.T, coupling, precision=highest)
    basis_term = jnp.dot(
        coupling.T, jnp.dot(basis_gram, coupling, precision=highest), precision=highest
    )
    spread = (
        diffused_gram
        - 2.0 * cross_term / samples_float
        + basis_term / (samples_float * samples_float)
    )
    factor = jnp.linalg.cholesky(spread)
    solved = jax.scipy.linalg.solve_triangular(factor, remainder, lower=True)
    return math.sqrt(samples_float) * solved


def solution(mesh):
    return jax.shard_map(
        per_device,
        mesh=mesh,
        in_specs=(P(None, ("row", "col")), P(("row", "col")), P(None, ("row", "col"))),
        out_specs=P(None, ("row", "col")),
        check_vma=False,
    )
```

profile of v0, /device:TPU:0, one launch (start us, length us, event | category | flops | bytes accessed | tf_op | source)
XLA Modules:
  0.0 157.3 jit_solution(3891402411580507994)
XLA Ops:
  6.5 0.0 reduce-scatter.9.cloned.1.call-start
  6.5 11.0 %all-gather.2 = bf16[8,192,32]{1,2,0:T(8,128)(2,1)S(1)} all-gather(bf16[1,192,32]{1,2,0:T(8,128)(2,1)} %bitcast.102), channel_id=1, replica_groups=mesh['row'=8,'col'=4] {'row'}, dimensions={0}, use_global_device_ids=true | all-gather | bytes 110592 | tf_op jit(solution)/shard_map/all_gather | solution.py:66
  17.5 13.6 %all-gather.1 = bf16[4,192,32]{1,2,0:T(8,128)(2,1)S(1)} all-gather(bf16[1,192,32]{1,2,0:T(8,128)(2,1)} %bitcast.103), channel_id=1, replica_groups=mesh['row'=8,'col'=4] {'col'}, dimensions={0}, use_global_device_ids=true | all-gather | bytes 61440 | tf_op jit(solution)/shard_map/all_gather | solution.py:61
  31.1 0.1 copy.27
  31.2 0.0 copy-start.2
  31.2 0.1 reshape.38
  31.4 0.1 copy.26
  31.4 0.1 reshape.36
  31.6 0.0 copy-done.1
  31.7 9.0 %all-gather.3 = bf16[8,192,32]{1,2,0:T(8,128)(2,1)S(1)} all-gather(bf16[1,192,32]{1,2,0:T(8,128)(2,1)S(1)} %fusion.17), channel_id=1, replica_groups=mesh['row'=8,'col'=4] {'row'}, dimensions={0}, use_global_device_ids=true | all-gather | bytes 110592 | tf_op jit(solution)/shard_map/all_gather | solution.py:67
  40.7 0.1 copy.28
  40.8 0.1 reshape.40
  40.9 0.6 dynamic-slice
  42.2 0.2 dynamic-update-slice.3
  42.4 13.2 %all-reduce = bf16[1536]{0:T(1024)(128)(2,1)S(1)} all-reduce(bf16[1536]{0:T(1024)(128)(2,1)S(1)} %dynamic-update-slice.3), channel_id=2, replica_groups=mesh['row'=8,'col'=4] {'row'}, use_global_device_ids=true, to_apply=%add | all-reduce | flops 1536 | bytes 6144
  55.6 3.6 %while.12 = (s32[]{:T(128)}, f32[3,32,256]{2,1,0:T(8,128)S(1)}, f32[3,1,256]{2,1,0:T(1,128)S(1)}, f32[3,256]{1,0:T(4,128)S(1)}, f32[1536]{0:T(1024)S(1)}, /*inde...) while((s32[]{:T(128)}, f32[3,32,256]{2,1,0:T(8,128)S(1)}, ...), condition=%wide.region_3.4_spmd, body=%wide.region_2.3_spmd.sunk | while | flops 53477376 | bytes 2623605 | solution.py:36
  55.7 0.5 fusion.52
  56.2 0.3 fusion.53
  56.5 0.3 fusion.54
  56.8 0.6 fusion.52
  57.4 0.3 fusion.53
  57.7 0.3 fusion.54
  58.0 0.6 fusion.52
  58.6 0.3 fusion.53
  58.9 0.3 fusion.54
  59.2 1.0 copy.40
  60.2 0.0 reduce-scatter.9.cloned.1.call-update
  60.2 0.0 reduce-scatter.7.cloned.1.call-start
  60.3 0.9 copy.42
  61.2 0.0 reduce-scatter.7.cloned.1.call-update
  61.2 0.2 fusion.19
  61.4 19.1 %reduce-scatter.9.cloned.1.call-done = f32[192,1]{1,0:T(8,128)} async-done(((f32[768,1]{1,0:T(8,128)}), f32[192,1]{1,0:T(8,128)}) %reduce-scatter.9.cloned.1.call-update) | async-done | bytes 784
  80.4 1.0 copy.41
  81.4 20.4 %reduce-scatter.7.cloned.1.call-done = f32[192,32]{1,0:T(8,128)} async-done(((f32[768,32]{1,0:T(8,128)}), f32[192,32]{1,0:T(8,128)}) %reduce-scatter.7.cloned.1.call-update) | async-done | bytes 24592
  101.8 1.0 copy.39
  102.8 0.2 fusion.18
  103.0 0.2 convolution_bitcast_fusion.2
  103.1 39.0 %all-reduce.1 = (f32[32,32]{0,1:T(8,128)S(1)}, f32[32,32]{0,1:T(8,128)S(1)}, f32[32,32]{1,0:T(8,128)S(1)}) all-reduce(f32[32,32]{0,1:T(8,128)S(1)} %convolution_bitcast_fusion.2, f32[32,32]{0,1:T(8,128)S(1)} %fusion.18, f32[32,32]{1,0:T(8,128)S(1)} %fusion.19), channel_id=1, replica_groups=mesh['row'=8,'col'=4] {'row','col'}, use_global_device_ids=true, to_apply=%region_7.8 | all-reduce | flops 3072 | bytes 24576 | tf_op jit(solution)/shard_map/psum | solution.py:78
  142.1 0.2 fusion.11
  142.3 0.1 fusion.20
  142.4 0.2 fusion.13
  142.6 0.2 fusion.12
  142.8 0.1 copy.34
  142.9 2.9 %cholesky.16 = f32[32,32]{1,0:T(8,128)S(1)} custom-call(f32[32,32]{1,0:T(8,128)S(1)} %fusion.16), custom_call_target="Cholesky" | custom-call | tf_op jit(solution)/shard_map/jit(cholesky)/cholesky | solution.py:96
  145.8 0.6 compare_reduce_fusion
  146.5 0.7 fusion.14
  147.1 2.4 %custom-call.7 = f32[1,32,32]{1,2,0:T(8,128)S(1)} custom-call(f32[1,32,32]{2,1,0:T(8,128)S(1)} %fusion.14), custom_call_target="InvertDiagBlocksLowerTriangular" | custom-call | tf_op jit(solution)/shard_map/jit(_solve_triangular)/triangular_solve | solution.py:97
  149.6 0.9 convolution_multiply_fusion.1
  (20 shorter events, 0.2 us)
Async XLA Ops:
  6.5 25.1 %copy-start.1 = (f32[192]{0:T(256)S(1)}, f32[192]{0:T(256)}, u32[]{:S(2)}) copy-start(f32[192]{0:T(256)} %param.6) | copy-start | bytes 2308
  6.5 25.1 %copy-start = (f32[32,192]{1,0:T(8,128)S(1)}, f32[32,192]{1,0:T(8,128)}, u32[]{:S(2)}) copy-start(f32[32,192]{1,0:T(8,128)} %param.7) | copy-start | bytes 73732
  6.5 73.9 %reduce-scatter.9.cloned.1.call-start = ((), (), s32[]{:S(2)}) async-start(), calls=%async_computation.3 | async-start | bytes 491520
  31.2 9.8 %copy-start.2 = (u32[32]{0:T(128)S(1)}, u32[32]{0:T(128)}, u32[]{:S(2)}) copy-start(u32[32]{0:T(128)} %constant.83) | copy-start | bytes 388
  60.2 41.6 %reduce-scatter.7.cloned.1.call-start = ((), (), s32[]{:S(2)}) async-start(), calls=%async_computation.2 | async-start | bytes 491520
Sparse Core Ops, SparseCore 0:
  60.3 20.0 reduce-scatter.8
  82.7 19.0 reduce-scatter.6
where the time goes:
time: 158 us; the launch traced here: 157 us
  blocking collectives  85.7 us (54%)
  waiting for transfers between devices  39.5 us (25%)
  between operations  14.2 us (9%)
  other arithmetic  6.76 us (4%)
  matrix products  5.55 us (4%)
  local copies, waits for them, and re-layouts  5.41 us (3%)
    unnamed x4, waiting for transfers between devices  39.5 us
    psum x1, blocking collectives, per_device(): lax.psum((jnp.dot(vectors, diffused.T, precision=highest), jnp.dot(diffus...  39 us
    all_gather x1, blocking collectives, per_device(): targets = lax.all_gather(descriptors, 'col', axis=1, tiled=True)  13.6 us
    unnamed x1, blocking collectives  13.2 us
    all_gather x1, blocking collectives, per_device(): lax.all_gather(descriptors, 'row', axis=1, tiled=True)  11 us
    all_gather x1, blocking collectives, per_device(): lax.all_gather(weighted, 'row', axis=1, tiled=True)  9.01 us
    unnamed x16, local copies, waits for them, and re-layouts  5.06 us
    another operation x3, other arithmetic, per_device(): factor = jnp.linalg.cholesky(spread)  3.6 us
  transfers between devices with their start and end apart: 2, of which 2 were waited for; matrix products, arithmetic and copies ran while one was open for 1% of the time, Pallas kernels for 0%

commit v1 on v0

v1 whole, which is shorter than its diff:
```python
import functools
import math

import jax
import jax.numpy as jnp
from jax import lax
from jax.experimental import pallas as pl
from jax.experimental.pallas import tpu as pltpu
from jax.sharding import PartitionSpec as P

kernel_width = 8.0
both_axes = ("row", "col")
highest = lax.Precision.HIGHEST
f32 = jnp.float32
bf16 = jnp.bfloat16
pad_rows = 8


def dot(a, b, contract, precision=None):
    return lax.dot_general(
        a, b, (contract, ((), ())), precision=precision, preferred_element_type=f32
    )


def split3(x):
    high = x.astype(bf16)
    rest = x - high.astype(f32)
    mid = rest.astype(bf16)
    low = (rest - mid.astype(f32)).astype(bf16)
    return high.astype(f32), mid.astype(f32), low.astype(f32)


def pack_kernel(desc_ref, dens_ref, vec_ref, out_ref):
    feat, count = desc_ref.shape
    vecs = vec_ref.shape[0]
    half = count // 3
    width = 2 * half
    desc = desc_ref[...]
    dens = dens_ref[...]
    weighted = (vec_ref[...] / dens).astype(bf16)
    inverse = (1.0 / dens).astype(bf16)
    out_ref[0:feat, :] = desc[:, :width]
    out_ref[feat : feat + vecs, :] = weighted[:, :width]
    base = feat + vecs
    out_ref[base : base + feat, :] = jnp.concatenate(
        [desc[:, width:], weighted[:, width:]], axis=1
    )
    base = base + feat
    tail = jnp.concatenate([inverse[:, width:], jnp.zeros((1, half), bf16)], axis=1)
    out_ref[base : base + pad_rows, :] = jnp.concatenate(
        [inverse[:, :width], tail, jnp.zeros((pad_rows - 2, width), bf16)], axis=0
    )


def target_rows(desc):
    values = desc.astype(f32)
    norm = jnp.sum(values * values, axis=0, keepdims=True)
    scale = -1.0 / kernel_width
    high, mid, low = split3(norm)
    ones = jnp.full_like(norm, scale)
    extra = jnp.concatenate(
        [ones, ones, ones, high * scale, mid * scale, low * scale, ones * 0.0, ones * 0.0],
        axis=0,
    )
    stacked = jnp.concatenate([values * (2.0 / kernel_width), extra], axis=0)
    return stacked.T.astype(bf16)


def source_columns(desc):
    values = desc.astype(f32)
    norm = jnp.sum(values * values, axis=0, keepdims=True)
    high, mid, low = split3(norm)
    ones = jnp.ones_like(norm)
    return jnp.concatenate(
        [values, high, mid, low, ones, ones, ones, ones * 0.0, ones * 0.0], axis=0
    ).astype(bf16)


def sums_kernel(packed_ref, own_ref, other_ref, own_out, other_out, *, vecs):
    feat, count = own_ref.shape
    pieces, _, width = packed_ref.shape
    half = count // 3
    rows = jnp.concatenate([target_rows(own_ref[...]), target_rows(other_ref[...])], axis=0)

    def step(pair, total):
        a = packed_ref[2 * pair]
        b = packed_ref[2 * pair + 1]
        base = feat + vecs
        desc = jnp.concatenate(
            [a[:feat], b[:feat], a[base : base + feat, :half], b[base : base + feat, :half]],
            axis=1,
        )
        weighted = jnp.concatenate(
            [a[feat:base], b[feat:base], a[base : base + feat, half:], b[base : base + feat, half:]],
            axis=1,
        )
        base = base + feat
        inverse = jnp.concatenate(
            [
                a[base : base + 1],
                b[base : base + 1],
                a[base + 1 : base + 2, :half],
                b[base + 1 : base + 2, :half],
            ],
            axis=1,
        )
        values = jnp.concatenate(
            [weighted.astype(f32), inverse.astype(f32), jnp.zeros((7, 2 * count), f32)], axis=0
        ).astype(bf16)
        exponent = dot(rows, source_columns(desc), ((1,), (0,)))
        kernel = jnp.exp(exponent).astype(bf16)
        return total + dot(kernel, values, ((1,), (1,)))

    total = lax.fori_loop(
        0, pieces // 2, step, jnp.zeros((2 * count, vecs + 8), f32), unroll=pieces <= 16
    )
    own_out[...] = total[:count].T
    other_out[...] = total[count:].T


def fold(matrix):
    side = matrix.shape[0]
    step = side // 4
    return jnp.concatenate([matrix[i * step : (i + 1) * step] for i in range(4)], axis=1)


def unfold(folded):
    step, width = folded.shape
    side = width // 4
    return jnp.concatenate([folded[:, i * side : (i + 1) * side] for i in range(4)], axis=0)


def gram_kernel(own_ref, got_ref, vec_ref, diffused_out, gram_out):
    vecs = vec_ref.shape[0]
    total = own_ref[...] + got_ref[...]
    diffused = total[:vecs] / total[vecs : vecs + 1]
    vectors = vec_ref[...]
    diffused_out[...] = diffused
    contract = ((1,), (1,))
    coupling = dot(vectors, diffused, contract, highest)
    diffused_gram = dot(diffused, diffused, contract, highest)
    basis_gram = dot(vectors, vectors, contract, highest)
    gram_out[...] = jnp.concatenate(
        [fold(coupling), fold(diffused_gram), fold(basis_gram)], axis=0
    )


def whiten_kernel(gram_ref, diffused_ref, vec_ref, out_ref, *, samples):
    vecs = vec_ref.shape[0]
    step = vecs // 4
    grams = gram_ref[...]
    coupling = unfold(grams[:step])
    diffused_gram = unfold(grams[step : 2 * step])
    basis_gram = unfold(grams[2 * step :])
    inner = dot(basis_gram, coupling, ((1,), (0,)), highest)
    mixed = (2.0 * coupling - inner / samples) / samples
    spread = diffused_gram - dot(coupling, mixed, ((0,), (0,)), highest)
    remainder = diffused_ref[...] - dot(coupling, vec_ref[...], ((0,), (0,)), highest) / samples
    table = spread
    solved = remainder
    row_index = lax.broadcasted_iota(jnp.int32, (vecs, 1), 0)
    for k in range(vecs):
        scale = lax.rsqrt(table[k : k + 1, k : k + 1])
        column = table[:, k : k + 1] * scale
        table_row = table[k : k + 1] * scale
        solved_row = solved[k : k + 1] * scale
        below = row_index > k
        at = row_index == k
        column = jnp.where(below, column, 0.0)
        table = table - column * table_row
        solved = jnp.where(at, solved_row, solved - column * solved_row)
    out_ref[...] = math.sqrt(samples) * solved


def whole(*shape_types):
    outs = tuple(jax.ShapeDtypeStruct(s, t) for s, t in shape_types)
    return outs if len(outs) > 1 else outs[0]


def local_call(body, outs, name, cost):
    return pl.pallas_call(
        body,
        out_shape=outs,
        name=name,
        cost_estimate=pl.CostEstimate(flops=cost, bytes_accessed=cost // 64, transcendentals=0),
    )


def per_device(rows, cols, descriptors, densities, vectors):
    feat, count = descriptors.shape
    vecs = vectors.shape[0]
    samples = float(count * rows * cols)
    devices = rows * cols

    def swap(x, mask):
        return lax.ppermute(x, both_axes, [(i, i ^ mask) for i in range(devices)])

    core_mask = cols
    col_masks = [1 << b for b in range(int(math.log2(cols)))]
    row_masks = [cols << b for b in range(1, int(math.log2(rows)))]
    width = 2 * (count // 3)
    height = 2 * feat + vecs + pad_rows

    other_desc = swap(descriptors, core_mask)
    packed = local_call(pack_kernel, whole(((height, width), bf16)), "pack", 1 << 16)(
        descriptors, densities[None, :], vectors
    )[None]
    for mask in col_masks[::-1] + row_masks:
        packed = jnp.concatenate([packed, swap(packed, mask)], axis=0)
    part = ((vecs + 8, count), f32)
    own, other = local_call(
        functools.partial(sums_kernel, vecs=vecs), whole(part, part), "sums", 1 << 30
    )(packed, descriptors, other_desc)
    got = swap(other, core_mask)
    diffused, grams = local_call(
        gram_kernel,
        whole(((vecs, count), f32), ((3 * vecs // 4, 4 * vecs), f32)),
        "gram",
        1 << 20,
    )(own, got, vectors)
    for mask in [core_mask] + row_masks + col_masks:
        grams = grams + swap(grams, mask)
    return local_call(
        functools.partial(whiten_kernel, samples=samples),
        whole(((vecs, count), f32)),
        "whiten",
        1 << 20,
    )(grams, diffused, vectors)


def solution(mesh):
    rows, cols = mesh.shape["row"], mesh.shape["col"]
    return jax.shard_map(
        functools.partial(per_device, rows, cols),
        mesh=mesh,
        in_specs=(P(None, both_axes), P(both_axes), P(None, both_axes)),
        out_specs=P(None, both_axes),
        check_vma=False,
    )
```

time: 158 us -> 55.6 us (0.35)
  blocking collectives: 85.7 us -> 0 us
  starting transfers between devices: 0.04 us -> 16.7 us
  waiting for transfers between devices: 39.5 us -> 23 us
  between operations: 14.2 us -> 0.06 us
  Pallas kernels: 0 us -> 11.2 us
  matrix products: 5.55 us -> 0 us
  other arithmetic: 6.76 us -> 2.11 us
  local copies, waits for them, and re-layouts: 5.41 us -> 2.03 us
    unnamed x4 -> x0, waiting for transfers between devices: 39.5 us -> none
    psum x1 -> x0, blocking collectives: 39 us -> none  [per_device(): lax.psum((jnp.dot(vectors, diffused.T, precision=highest), jnp.dot(diffus...]
    all_gather x3 -> x0, blocking collectives: 33.6 us -> none  [the longest x1 13.6 us: per_device(): targets = lax.all_gather(descriptors, 'col', axis=1, tiled=True)]
    ppermute x0 -> x11, waiting for transfers between devices: none -> 23 us  [swap(): return lax.ppermute(x, both_axes, [(i, i ^ mask) for i in range(devices)])]
    ppermute x0 -> x11, starting transfers between devices: none -> 16.7 us  [swap(): return lax.ppermute(x, both_axes, [(i, i ^ mask) for i in range(devices)])]
    unnamed x1 -> x0, blocking collectives: 13.2 us -> none
    pallas_call x0 -> x4, Pallas kernels: none -> 11.2 us  [the longest x1 4.42 us: per_device(): local_call(functools.partial(whiten_kernel, samples=samples), whole(((vec...]
    another operation x5 -> x0, other arithmetic: 6.68 us -> none  [the longest x3 3.6 us: per_device(): factor = jnp.linalg.cholesky(spread)]
  transfers between devices with their start and end apart: 2 -> 11, of which waited for: 2 -> 10; matrix products, arithmetic and copies ran while one was open for 1% -> 2% of each run, Pallas kernels for 0% -> 0%
where the time goes in v1:
time: 55.6 us; the launch traced here: 55.1 us
  waiting for transfers between devices  23 us (41%)
  starting transfers between devices  16.7 us (30%)
  Pallas kernels  11.2 us (20%)
  other arithmetic  2.11 us (4%)
  local copies, waits for them, and re-layouts  2.03 us (4%)
    ppermute x11, waiting for transfers between devices, swap(): return lax.ppermute(x, both_axes, [(i, i ^ mask) for i in range(devices)])  23 us
    ppermute x11, starting transfers between devices, swap(): return lax.ppermute(x, both_axes, [(i, i ^ mask) for i in range(devices)])  16.7 us
    pallas_call x1, Pallas kernels, per_device(): local_call(functools.partial(whiten_kernel, samples=samples), whole(((vec...  4.42 us
    pallas_call x1, Pallas kernels, per_device(): local_call(functools.partial(sums_kernel, vecs=vecs), whole(part, part),...  3.61 us
    unnamed x14, local copies, waits for them, and re-layouts  2 us
    pallas_call x1, Pallas kernels, per_device(): local_call(gram_kernel, whole(((vecs, count), f32), ((3 * vecs // 4, 4 *...  1.7 us
    pallas_call x1, Pallas kernels, per_device(): local_call(pack_kernel, whole(((height, width), bf16)), 'pack', 1 << 16)  1.49 us
    add x5, other arithmetic, per_device(): grams = grams + swap(grams, mask)  1.33 us
  transfers between devices with their start and end apart: 11, of which 10 were waited for; matrix products, arithmetic and copies ran while one was open for 2% of the time, Pallas kernels for 0%

profile of v1, /device:TPU:0, one launch (start us, length us, event | category | flops | bytes accessed | tf_op | source)
XLA Modules:
  0.0 55.1 jit_solution(1870271881861868832)
XLA Ops:
  0.0 0.0 copy-start.2
  0.0 1.5 %pack.1 = bf16[104,128]{1,0:T(8,128)(2,1)} custom-call(bf16[32,192]{1,0:T(8,128)(2,1)} %own_ref.1, f32[1,192]{1,0:T(1,128)} %bitcast.7, f32[32,192]{1,0:T(8,128)} %vec_ref.5), custom_call_target="tpu_custom_call" | custom-call | flops 65536 | bytes 1024 | tf_op jit(solution)/shard_map/pack/pallas_call | solution.py:205
  1.5 0.0 copy-start
  1.5 4.1 %collective-permute-start = (bf16[1,104,128]{2,1,0:T(8,128)(2,1)}, bf16[1,104,128]{2,1,0:T(8,128)(2,1)S(1)}, u32[]{:S(2)}, u32[]{:S(2)}) collective-permute-start(bf16[1,104,128]{2,1,0:T(8,128)(2,1)} %bitcast.3), channel_id=1, source_target_pairs={{0,2},{1,3},{2,0},{3,1},{4,6},{5,7},{6,4},{7,5},{8,10},{9,11},{10,... | collective-permute-start | bytes 79880 | tf_op jit(solution)/shard_map/ppermute | solution.py:196
  5.6 0.0 copy-done.2
  5.6 0.0 collective-permute-start.4
  5.6 2.4 %collective-permute-done = bf16[1,104,128]{2,1,0:T(8,128)(2,1)S(1)} collective-permute-done((bf16[1,104,128]{2,1,0:T(8,128)(2,1)}, bf16[1,104,128]{2,1,0:T(8,128)(2,1)S(1)}, u32[]{:S(2)}, u32[]{:S(2)}) %collective-permute-start) | collective-permute-done | bytes 26656 | tf_op jit(solution)/shard_map/ppermute | solution.py:196
  8.0 0.7 %pad_maximum_fusion.2 = bf16[2,104,128]{2,1,0:T(8,128)(2,1)S(1)} fusion(bf16[1,104,128]{2,1,0:T(8,128)(2,1)S(1)} %collective-permute-done, bf16[1,104,128]{2,1,0:T(8,128)(2,1)} %bitcast.4), kind=kLoop, calls=%fused_computation.2 | loop fusion | flops 26624 | bytes 106496 | tf_op jit(solution)/shard_map/concatenate | solution.py:209
  8.7 1.6 %collective-permute-start.1 = (bf16[2,104,128]{2,1,0:T(8,128)(2,1)S(1)}, bf16[2,104,128]{2,1,0:T(8,128)(2,1)S(1)}, u32[]{:S(2)}, u32[]{:S(2)}) collective-permute-start(bf16[2,104,128]{2,1,0:T(8,128)(2,1)S(1)} %pad_maximum_fusion.2), channel_id=1, source_target_pairs={{0,1},{1,0},{2,3},{3,2},{4,5},{5,4},{6,7},{7,6},{8,9},{9,8},{10,11... | collective-permute-start | bytes 159752 | tf_op jit(solution)/shard_map/ppermute | solution.py:196
  10.3 0.0 copy-done
  10.3 2.6 %collective-permute-done.1 = bf16[2,104,128]{2,1,0:T(8,128)(2,1)S(1)} collective-permute-done((bf16[2,104,128]{2,1,0:T(8,128)(2,1)S(1)}, bf16[2,104,128]{2,1,0:T(8,128)(2,1)S(1)}, u32[]{:S(2)}, u32[]{:S(2)}) %collective-permute-start.1) | collective-permute-done | bytes 53280 | tf_op jit(solution)/shard_map/ppermute | solution.py:196
  12.9 1.7 %collective-permute-start.2 = (bf16[4,104,128]{2,1,0:T(8,128)(2,1)S(1)}, bf16[4,104,128]{2,1,0:T(8,128)(2,1)S(1)}, u32[]{:S(2)}, u32[]{:S(2)}) collective-permute-start(bf16[4,104,128]{2,1,0:T(8,128)(2,1)S(1)} %pad_maximum_fusion.1), channel_id=1, source_target_pairs={{0,8},{1,9},{2,10},{3,11},{4,12},{5,13},{6,14},{7,15},{8,0},{9,1},... | collective-permute-start | bytes 319496 | tf_op jit(solution)/shard_map/ppermute | solution.py:196
  14.6 3.0 %collective-permute-done.2 = bf16[4,104,128]{2,1,0:T(8,128)(2,1)S(1)} collective-permute-done((bf16[4,104,128]{2,1,0:T(8,128)(2,1)S(1)}, bf16[4,104,128]{2,1,0:T(8,128)(2,1)S(1)}, u32[]{:S(2)}, u32[]{:S(2)}) %collective-permute-start.2) | collective-permute-done | bytes 106528 | tf_op jit(solution)/shard_map/ppermute | solution.py:196
  17.7 1.7 %collective-permute-start.3 = (bf16[8,104,128]{2,1,0:T(8,128)(2,1)S(1)}, bf16[8,104,128]{2,1,0:T(8,128)(2,1)S(1)}, u32[]{:S(2)}, u32[]{:S(2)}) collective-permute-start(bf16[8,104,128]{2,1,0:T(8,128)(2,1)S(1)} %pad_maximum_fusion), channel_id=1, source_target_pairs={{0,16},{1,17},{2,18},{3,19},{4,20},{5,21},{6,22},{7,23},{8,24},{9,... | collective-permute-start | bytes 638984 | tf_op jit(solution)/shard_map/ppermute | solution.py:196
  19.4 4.1 %collective-permute-done.3 = bf16[8,104,128]{2,1,0:T(8,128)(2,1)S(1)} collective-permute-done((bf16[8,104,128]{2,1,0:T(8,128)(2,1)S(1)}, bf16[8,104,128]{2,1,0:T(8,128)(2,1)S(1)}, u32[]{:S(2)}, u32[]{:S(2)}) %collective-permute-start.3) | collective-permute-done | bytes 213024 | tf_op jit(solution)/shard_map/ppermute | solution.py:196
  23.6 0.0 copy-start.3
  23.6 0.0 collective-permute-done.4.other_ref
  23.6 0.7 %copy-done.3 = bf16[16,104,128]{2,1,0:T(8,128)(2,1)} copy-done((bf16[16,104,128]{2,1,0:T(8,128)(2,1)}, bf16[16,104,128]{2,1,0:T(8,128)(2,1)S(1)}, u32[]{:S(2)}) %copy-start.3) | copy-done | bytes 426008
  24.4 0.0 copy-start.4
  24.4 0.6 %copy-done.4 = bf16[32,192]{1,0:T(8,128)(2,1)} copy-done((bf16[32,192]{1,0:T(8,128)(2,1)}, bf16[32,192]{1,0:T(8,128)(2,1)S(1)}, u32[]{:S(2)}) %copy-start.4) | copy-done | bytes 12312
  25.0 3.6 %sums.1 = (f32[40,192]{1,0:T(8,128)}, f32[40,192]{1,0:T(8,128)}) custom-call(bf16[16,104,128]{2,1,0:T(8,128)(2,1)} %copy-done.3, bf16[32,192]{1,0:T(8,128)(2,1)} %own_ref.1, bf16[32,192]{1,0:T(8,128)(2,1)} %copy-done.4), custom_call_target="tpu_custom_call" | custom-call | flops 1073741824 | bytes 16777216 | tf_op jit(solution)/shard_map/sums/pallas_call | solution.py:211
  28.6 0.0 collective-permute-start.5
  28.6 1.4 %collective-permute-done.5.got_ref = f32[40,192]{1,0:T(8,128)S(1)} collective-permute-done((f32[40,192]{1,0:T(8,128)}, f32[40,192]{1,0:T(8,128)S(1)}, u32[]{:S(2)}, u32[]{:S(2)}) %collective-permute-start.5) | collective-permute-done | bytes 30752 | tf_op jit(solution)/shard_map/ppermute | solution.py:196
  30.0 0.0 copy-start.1
  30.0 0.6 %copy-done.1 = f32[40,192]{1,0:T(8,128)} copy-done((f32[40,192]{1,0:T(8,128)}, f32[40,192]{1,0:T(8,128)S(1)}, u32[]{:S(2)}) %copy-start.1) | copy-done | bytes 30744
  30.6 1.7 %gram.1 = (f32[32,192]{1,0:T(8,128)}, f32[24,128]{1,0:T(8,128)}) custom-call(f32[40,192]{1,0:T(8,128)} %get-tuple-element.9.own_ref, f32[40,192]{1,0:T(8,128)} %copy-done.1, f32[32,192]{1,0:T(8,128)} %vec_ref.5), custom_call_target="tpu_custom_call" | custom-call | flops 1048576 | bytes 16384 | tf_op jit(solution)/shard_map/gram/pallas_call | solution.py:215
  32.3 0.2 collective-permute-start.6
  32.5 1.2 %collective-permute-done.6 = f32[24,128]{1,0:T(8,128)S(1)} collective-permute-done((f32[24,128]{1,0:T(8,128)}, f32[24,128]{1,0:T(8,128)S(1)}, u32[]{:S(2)}, u32[]{:S(2)}) %collective-permute-start.6) | collective-permute-done | bytes 12320 | tf_op jit(solution)/shard_map/ppermute | solution.py:196
  33.7 0.7 %add.15 = f32[24,128]{1,0:T(8,128)S(1)} add(f32[24,128]{1,0:T(8,128)} %get-tuple-element.11, f32[24,128]{1,0:T(8,128)S(1)} %collective-permute-done.6) | non-fusion elementwise | flops 3072 | bytes 36864 | tf_op jit(solution)/shard_map/add | solution.py:222
  34.4 1.6 %collective-permute-start.7 = (f32[24,128]{1,0:T(8,128)S(1)}, f32[24,128]{1,0:T(8,128)S(1)}, u32[]{:S(2)}, u32[]{:S(2)}) collective-permute-start(f32[24,128]{1,0:T(8,128)S(1)} %add.15), channel_id=1, source_target_pairs={{0,8},{1,9},{2,10},{3,11},{4,12},{5,13},{6,14},{7,15},{8,0},{9,1},... | collective-permute-start | bytes 36872 | tf_op jit(solution)/shard_map/ppermute | solution.py:196
  36.1 2.0 %collective-permute-done.7 = f32[24,128]{1,0:T(8,128)S(1)} collective-permute-done((f32[24,128]{1,0:T(8,128)S(1)}, f32[24,128]{1,0:T(8,128)S(1)}, u32[]{:S(2)}, u32[]{:S(2)}) %collective-permute-start.7) | collective-permute-done | bytes 12320 | tf_op jit(solution)/shard_map/ppermute | solution.py:196
  38.1 1.7 %collective-permute-start.8 = (f32[24,128]{1,0:T(8,128)S(1)}, f32[24,128]{1,0:T(8,128)S(1)}, u32[]{:S(2)}, u32[]{:S(2)}) collective-permute-start(f32[24,128]{1,0:T(8,128)S(1)} %add.16), channel_id=1, source_target_pairs={{0,16},{1,17},{2,18},{3,19},{4,20},{5,21},{6,22},{7,23},{8,24},{9,... | collective-permute-start | bytes 36872 | tf_op jit(solution)/shard_map/ppermute | solution.py:196
  39.8 2.0 %collective-permute-done.8 = f32[24,128]{1,0:T(8,128)S(1)} collective-permute-done((f32[24,128]{1,0:T(8,128)S(1)}, f32[24,128]{1,0:T(8,128)S(1)}, u32[]{:S(2)}, u32[]{:S(2)}) %collective-permute-start.8) | collective-permute-done | bytes 12320 | tf_op jit(solution)/shard_map/ppermute | solution.py:196
  41.8 1.6 %collective-permute-start.9 = (f32[24,128]{1,0:T(8,128)S(1)}, f32[24,128]{1,0:T(8,128)S(1)}, u32[]{:S(2)}, u32[]{:S(2)}) collective-permute-start(f32[24,128]{1,0:T(8,128)S(1)} %add.17), channel_id=1, source_target_pairs={{0,1},{1,0},{2,3},{3,2},{4,5},{5,4},{6,7},{7,6},{8,9},{9,8},{10,11... | collective-permute-start | bytes 36872 | tf_op jit(solution)/shard_map/ppermute | solution.py:196
  43.4 2.1 %collective-permute-done.9 = f32[24,128]{1,0:T(8,128)S(1)} collective-permute-done((f32[24,128]{1,0:T(8,128)S(1)}, f32[24,128]{1,0:T(8,128)S(1)}, u32[]{:S(2)}, u32[]{:S(2)}) %collective-permute-start.9) | collective-permute-done | bytes 12320 | tf_op jit(solution)/shard_map/ppermute | solution.py:196
  45.5 2.6 %collective-permute-start.10 = (f32[24,128]{1,0:T(8,128)S(1)}, f32[24,128]{1,0:T(8,128)S(1)}, u32[]{:S(2)}, u32[]{:S(2)}) collective-permute-start(f32[24,128]{1,0:T(8,128)S(1)} %add.18), channel_id=1, source_target_pairs={{0,2},{1,3},{2,0},{3,1},{4,6},{5,7},{6,4},{7,5},{8,10},{9,11},{10,... | collective-permute-start | bytes 36872 | tf_op jit(solution)/shard_map/ppermute | solution.py:196
  48.1 2.0 %collective-permute-done.10 = f32[24,128]{1,0:T(8,128)S(1)} collective-permute-done((f32[24,128]{1,0:T(8,128)S(1)}, f32[24,128]{1,0:T(8,128)S(1)}, u32[]{:S(2)}, u32[]{:S(2)}) %collective-permute-start.10) | collective-permute-done | bytes 12320 | tf_op jit(solution)/shard_map/ppermute | solution.py:196
  50.1 0.6 %add.19.gram_ref = f32[24,128]{1,0:T(8,128)} add(f32[24,128]{1,0:T(8,128)S(1)} %add.18, f32[24,128]{1,0:T(8,128)S(1)} %collective-permute-done.10) | non-fusion elementwise | flops 3072 | bytes 36864 | tf_op jit(solution)/shard_map/add | solution.py:222
  50.7 4.4 %whiten.1 = f32[32,192]{1,0:T(8,128)} custom-call(f32[24,128]{1,0:T(8,128)} %add.19.gram_ref, f32[32,192]{1,0:T(8,128)} %get-tuple-element.12.diffused_ref, f32[32,192]{1,0:T(8,128)} %vec_ref.5), custom_call_target="tpu_custom_call" | custom-call | flops 1048576 | bytes 16384 | tf_op jit(solution)/shard_map/whiten/pallas_call | solution.py:223
  (10 shorter events, 0.1 us)
Async XLA Ops:
  0.0 5.6 %copy-start.2 = (bf16[32,192]{1,0:T(8,128)(2,1)S(1)}, bf16[32,192]{1,0:T(8,128)(2,1)}, u32[]{:S(2)}) copy-start(bf16[32,192]{1,0:T(8,128)(2,1)} %own_ref.1) | copy-start | bytes 36868
  1.5 8.8 %copy-start = (bf16[104,128]{1,0:T(8,128)(2,1)S(1)}, bf16[104,128]{1,0:T(8,128)(2,1)}, u32[]{:S(2)}) copy-start(bf16[104,128]{1,0:T(8,128)(2,1)} %pack.1) | copy-start | bytes 79876
  1.5 6.5 %collective-permute-start = (bf16[1,104,128]{2,1,0:T(8,128)(2,1)}, bf16[1,104,128]{2,1,0:T(8,128)(2,1)S(1)}, u32[]{:S(2)}, u32[]{:S(2)}) collective-permute-start(bf16[1,104,128]{2,1,0:T(8,128)(2,1)} %bitcast.3), channel_id=1, source_target_pairs={{0,2},{1,3},{2,0},{3,1},{4,6},{5,7},{6,4},{7,5},{8,10},{9,11},{10,... | collective-permute-start | bytes 79880 | tf_op jit(solution)/shard_map/ppermute | solution.py:196
  5.6 18.0 %collective-permute-start.4 = (bf16[32,192]{1,0:T(8,128)(2,1)S(1)}, bf16[32,192]{1,0:T(8,128)(2,1)S(1)}, u32[]{:S(2)}, u32[]{:S(2)}) collective-permute-start(bf16[32,192]{1,0:T(8,128)(2,1)S(1)} %copy-done.2), channel_id=1, source_target_pairs={{0,4},{1,5},{2,6},{3,7},{4,0},{5,1},{6,2},{7,3},{8,12},{9,13},{10,... | collective-permute-start | bytes 36872 | tf_op jit(solution)/shard_map/ppermute | solution.py:196
  8.7 4.1 %collective-permute-start.1 = (bf16[2,104,128]{2,1,0:T(8,128)(2,1)S(1)}, bf16[2,104,128]{2,1,0:T(8,128)(2,1)S(1)}, u32[]{:S(2)}, u32[]{:S(2)}) collective-permute-start(bf16[2,104,128]{2,1,0:T(8,128)(2,1)S(1)} %pad_maximum_fusion.2), channel_id=1, source_target_pairs={{0,1},{1,0},{2,3},{3,2},{4,5},{5,4},{6,7},{7,6},{8,9},{9,8},{10,11... | collective-permute-start | bytes 159752 | tf_op jit(solution)/shard_map/ppermute | solution.py:196
  12.9 4.8 %collective-permute-start.2 = (bf16[4,104,128]{2,1,0:T(8,128)(2,1)S(1)}, bf16[4,104,128]{2,1,0:T(8,128)(2,1)S(1)}, u32[]{:S(2)}, u32[]{:S(2)}) collective-permute-start(bf16[4,104,128]{2,1,0:T(8,128)(2,1)S(1)} %pad_maximum_fusion.1), channel_id=1, source_target_pairs={{0,8},{1,9},{2,10},{3,11},{4,12},{5,13},{6,14},{7,15},{8,0},{9,1},... | collective-permute-start | bytes 319496 | tf_op jit(solution)/shard_map/ppermute | solution.py:196
  17.7 5.9 %collective-permute-start.3 = (bf16[8,104,128]{2,1,0:T(8,128)(2,1)S(1)}, bf16[8,104,128]{2,1,0:T(8,128)(2,1)S(1)}, u32[]{:S(2)}, u32[]{:S(2)}) collective-permute-start(bf16[8,104,128]{2,1,0:T(8,128)(2,1)S(1)} %pad_maximum_fusion), channel_id=1, source_target_pairs={{0,16},{1,17},{2,18},{3,19},{4,20},{5,21},{6,22},{7,23},{8,24},{9,... | collective-permute-start | bytes 638984 | tf_op jit(solution)/shard_map/ppermute | solution.py:196
  23.6 0.8 %copy-start.3 = (bf16[16,104,128]{2,1,0:T(8,128)(2,1)}, bf16[16,104,128]{2,1,0:T(8,128)(2,1)S(1)}, u32[]{:S(2)}) copy-start(bf16[16,104,128]{2,1,0:T(8,128)(2,1)S(1)} %constant_dynamic-update-slice_fusion.packed_ref) | copy-start | bytes 1277956
  24.4 0.6 %copy-start.4 = (bf16[32,192]{1,0:T(8,128)(2,1)}, bf16[32,192]{1,0:T(8,128)(2,1)S(1)}, u32[]{:S(2)}) copy-start(bf16[32,192]{1,0:T(8,128)(2,1)S(1)} %collective-permute-done.4.other_ref) | copy-start | bytes 36868
  28.6 1.4 %collective-permute-start.5 = (f32[40,192]{1,0:T(8,128)}, f32[40,192]{1,0:T(8,128)S(1)}, u32[]{:S(2)}, u32[]{:S(2)}) collective-permute-start(f32[40,192]{1,0:T(8,128)} %get-tuple-element.10), channel_id=1, source_target_pairs={{0,4},{1,5},{2,6},{3,7},{4,0},{5,1},{6,2},{7,3},{8,12},{9,13},{10,... | collective-permute-start | bytes 92168 | tf_op jit(solution)/shard_map/ppermute | solution.py:196
  30.0 0.6 %copy-start.1 = (f32[40,192]{1,0:T(8,128)}, f32[40,192]{1,0:T(8,128)S(1)}, u32[]{:S(2)}) copy-start(f32[40,192]{1,0:T(8,128)S(1)} %collective-permute-done.5.got_ref) | copy-start | bytes 92164
  32.3 1.4 %collective-permute-start.6 = (f32[24,128]{1,0:T(8,128)}, f32[24,128]{1,0:T(8,128)S(1)}, u32[]{:S(2)}, u32[]{:S(2)}) collective-permute-start(f32[24,128]{1,0:T(8,128)} %get-tuple-element.11), channel_id=1, source_target_pairs={{0,4},{1,5},{2,6},{3,7},{4,0},{5,1},{6,2},{7,3},{8,12},{9,13},{10,... | collective-permute-start | bytes 36872 | tf_op jit(solution)/shard_map/ppermute | solution.py:196
  34.4 3.7 %collective-permute-start.7 = (f32[24,128]{1,0:T(8,128)S(1)}, f32[24,128]{1,0:T(8,128)S(1)}, u32[]{:S(2)}, u32[]{:S(2)}) collective-permute-start(f32[24,128]{1,0:T(8,128)S(1)} %add.15), channel_id=1, source_target_pairs={{0,8},{1,9},{2,10},{3,11},{4,12},{5,13},{6,14},{7,15},{8,0},{9,1},... | collective-permute-start | bytes 36872 | tf_op jit(solution)/shard_map/ppermute | solution.py:196
  38.1 3.7 %collective-permute-start.8 = (f32[24,128]{1,0:T(8,128)S(1)}, f32[24,128]{1,0:T(8,128)S(1)}, u32[]{:S(2)}, u32[]{:S(2)}) collective-permute-start(f32[24,128]{1,0:T(8,128)S(1)} %add.16), channel_id=1, source_target_pairs={{0,16},{1,17},{2,18},{3,19},{4,20},{5,21},{6,22},{7,23},{8,24},{9,... | collective-permute-start | bytes 36872 | tf_op jit(solution)/shard_map/ppermute | solution.py:196
  41.8 3.7 %collective-permute-start.9 = (f32[24,128]{1,0:T(8,128)S(1)}, f32[24,128]{1,0:T(8,128)S(1)}, u32[]{:S(2)}, u32[]{:S(2)}) collective-permute-start(f32[24,128]{1,0:T(8,128)S(1)} %add.17), channel_id=1, source_target_pairs={{0,1},{1,0},{2,3},{3,2},{4,5},{5,4},{6,7},{7,6},{8,9},{9,8},{10,11... | collective-permute-start | bytes 36872 | tf_op jit(solution)/shard_map/ppermute | solution.py:196
  45.5 4.6 %collective-permute-start.10 = (f32[24,128]{1,0:T(8,128)S(1)}, f32[24,128]{1,0:T(8,128)S(1)}, u32[]{:S(2)}, u32[]{:S(2)}) collective-permute-start(f32[24,128]{1,0:T(8,128)S(1)} %add.18), channel_id=1, source_target_pairs={{0,2},{1,3},{2,0},{3,1},{4,6},{5,7},{6,4},{7,5},{8,10},{9,11},{10,... | collective-permute-start | bytes 36872 | tf_op jit(solution)/shard_map/ppermute | solution.py:196

commit v2 on v1

--- a/solution.py
+++ b/solution.py
@@ -177,11 +177,15 @@
     return outs if len(outs) > 1 else outs[0]
 
 
-def local_call(body, outs, name, cost):
+def local_call(body, outs, name, cost, args, grant=4):
+    vmem = pl.BlockSpec(memory_space=pltpu.VMEM)
     return pl.pallas_call(
         body,
         out_shape=outs,
         name=name,
+        in_specs=[vmem] * args,
+        out_specs=jax.tree.map(lambda _: vmem, outs),
+        compiler_params=pltpu.CompilerParams(vmem_limit_bytes=grant << 20),
         cost_estimate=pl.CostEstimate(flops=cost, bytes_accessed=cost // 64, transcendentals=0),
     )
 
@@ -202,14 +206,14 @@
     height = 2 * feat + vecs + pad_rows
 
     other_desc = swap(descriptors, core_mask)
-    packed = local_call(pack_kernel, whole(((height, width), bf16)), "pack", 1 << 16)(
+    packed = local_call(pack_kernel, whole(((height, width), bf16)), "pack", 1 << 16, 3)(
         descriptors, densities[None, :], vectors
     )[None]
     for mask in col_masks[::-1] + row_masks:
         packed = jnp.concatenate([packed, swap(packed, mask)], axis=0)
     part = ((vecs + 8, count), f32)
     own, other = local_call(
-        functools.partial(sums_kernel, vecs=vecs), whole(part, part), "sums", 1 << 30
+        functools.partial(sums_kernel, vecs=vecs), whole(part, part), "sums", 1 << 30, 3, 16
     )(packed, descriptors, other_desc)
     got = swap(other, core_mask)
     diffused, grams = local_call(
@@ -217,6 +221,7 @@
         whole(((vecs, count), f32), ((3 * vecs // 4, 4 * vecs), f32)),
         "gram",
         1 << 20,
+        3,
     )(own, got, vectors)
     for mask in [core_mask] + row_masks + col_masks:
         grams = grams + swap(grams, mask)
@@ -225,6 +230,7 @@
         whole(((vecs, count), f32)),
         "whiten",
         1 << 20,
+        3,
     )(grams, diffused, vectors)
 
 

time: 55.6 us -> 48.2 us (0.87)
  Pallas kernels: 11.2 us -> 7.36 us
  waiting for transfers between devices: 23 us -> 19.7 us
  starting transfers between devices: 16.7 us -> 19.2 us
  other arithmetic: 2.11 us -> 0.06 us
    ppermute x11, waiting for transfers between devices: 23 us -> 19.7 us  [swap(): return lax.ppermute(x, both_axes, [(i, i ^ mask) for i in range(devices)])]
    ppermute x11, starting transfers between devices: 16.7 us -> 19.2 us  [swap(): return lax.ppermute(x, both_axes, [(i, i ^ mask) for i in range(devices)])]
    pallas_call x1, Pallas kernels: 1.7 us -> 0.24 us  [per_device(): local_call(gram_kernel, whole(((vecs, count), f32), ((3 * vecs // 4, 4 *...]
    add x5, other arithmetic: 1.33 us -> 0.02 us  [per_device(): grams = grams + swap(grams, mask)]
    pallas_call x1, Pallas kernels: 3.61 us -> 2.69 us  [per_device(): local_call(functools.partial(sums_kernel, vecs=vecs), whole(part, part),...]
    pallas_call x1, Pallas kernels: 4.42 us -> 3.63 us  [per_device(): local_call(functools.partial(whiten_kernel, samples=samples), whole(((vec...]
    concatenate x3, other arithmetic: 0.79 us -> 0.04 us  [per_device(): packed = jnp.concatenate([packed, swap(packed, mask)], axis=0)]
    pallas_call x1, Pallas kernels: 1.49 us -> 0.8 us  [per_device(): local_call(pack_kernel, whole(((height, width), bf16)), 'pack', 1 << 16, 3)]
  transfers between devices with their start and end apart: 11 -> 11, of which waited for: 10 -> 10; matrix products, arithmetic and copies ran while one was open for 2% -> 0% of each run, Pallas kernels for 0% -> 0%
where the time goes in v2:
time: 48.2 us; the launch traced here: 47.9 us
  waiting for transfers between devices  19.7 us (41%)
  starting transfers between devices  19.2 us (40%)
  Pallas kernels  7.36 us (15%)
  local copies, waits for them, and re-layouts  1.51 us (3%)
    ppermute x11, waiting for transfers between devices, swap(): return lax.ppermute(x, both_axes, [(i, i ^ mask) for i in range(devices)])  19.7 us
    ppermute x11, starting transfers between devices, swap(): return lax.ppermute(x, both_axes, [(i, i ^ mask) for i in range(devices)])  19.2 us
    pallas_call x1, Pallas kernels, per_device(): local_call(functools.partial(whiten_kernel, samples=samples), whole(((vec...  3.63 us
    pallas_call x1, Pallas kernels, per_device(): local_call(functools.partial(sums_kernel, vecs=vecs), whole(part, part),...  2.69 us
    unnamed x10, local copies, waits for them, and re-layouts  1.48 us
  transfers between devices with their start and end apart: 11, of which 10 were waited for; matrix products, arithmetic and copies ran while one was open for 0% of the time, Pallas kernels for 0%

profile of v2, /device:TPU:0, one launch (start us, length us, event | category | flops | bytes accessed | tf_op | source)
XLA Modules:
  0.0 47.9 jit_solution(15505310217609194290)
XLA Ops:
  0.0 0.0 copy-start.2
  0.0 0.7 %copy-done.2 = f32[192]{0:T(256)S(1)} copy-done((f32[192]{0:T(256)S(1)}, f32[192]{0:T(256)}, u32[]{:S(2)}) %copy-start.2) | copy-done | bytes 792
  0.7 0.0 copy-start
  0.7 0.8 %copy-done = f32[32,192]{1,0:T(8,128)S(1)} copy-done((f32[32,192]{1,0:T(8,128)S(1)}, f32[32,192]{1,0:T(8,128)}, u32[]{:S(2)}) %copy-start) | copy-done | bytes 24600
  1.4 0.8 %pack.1 = bf16[104,128]{1,0:T(8,128)(2,1)S(1)} custom-call(bf16[32,192]{1,0:T(8,128)(2,1)} %own_ref.1, f32[1,192]{1,0:T(1,128)S(1)} %bitcast.7, f32[32,192]{1,0:T(8,128)S(1)} %copy-done), custom_call_target="tpu_custom_call" | custom-call | flops 65536 | bytes 1024 | tf_op jit(solution)/shard_map/pack/pallas_call | solution.py:209
  2.2 4.1 %collective-permute-start = (bf16[1,104,128]{2,1,0:T(8,128)(2,1)S(1)}, bf16[1,104,128]{2,1,0:T(8,128)(2,1)S(1)}, u32[]{:S(2)}, u32[]{:S(2)}) collective-permute-start(bf16[1,104,128]{2,1,0:T(8,128)(2,1)S(1)} %bitcast.3), channel_id=1, source_target_pairs={{0,2},{1,3},{2,0},{3,1},{4,6},{5,7},{6,4},{7,5},{8,10},{9,11},{10,... | collective-permute-start | bytes 79880 | tf_op jit(solution)/shard_map/ppermute | solution.py:200
  6.3 0.0 collective-permute-start.4
  6.3 1.8 %collective-permute-done = bf16[1,104,128]{2,1,0:T(8,128)(2,1)S(1)} collective-permute-done((bf16[1,104,128]{2,1,0:T(8,128)(2,1)S(1)}, bf16[1,104,128]{2,1,0:T(8,128)(2,1)S(1)}, u32[]{:S(2)}, u32[]{:S(2)}) %collective-permute-start) | collective-permute-done | bytes 26656 | tf_op jit(solution)/shard_map/ppermute | solution.py:200
  8.2 2.0 %collective-permute-start.1 = (bf16[2,104,128]{2,1,0:T(8,128)(2,1)S(1)}, bf16[2,104,128]{2,1,0:T(8,128)(2,1)S(1)}, u32[]{:S(2)}, u32[]{:S(2)}) collective-permute-start(bf16[2,104,128]{2,1,0:T(8,128)(2,1)S(1)} %pad_maximum_fusion.2), channel_id=1, source_target_pairs={{0,1},{1,0},{2,3},{3,2},{4,5},{5,4},{6,7},{7,6},{8,9},{9,8},{10,11... | collective-permute-start | bytes 159752 | tf_op jit(solution)/shard_map/ppermute | solution.py:200
  10.1 2.2 %collective-permute-done.1 = bf16[2,104,128]{2,1,0:T(8,128)(2,1)S(1)} collective-permute-done((bf16[2,104,128]{2,1,0:T(8,128)(2,1)S(1)}, bf16[2,104,128]{2,1,0:T(8,128)(2,1)S(1)}, u32[]{:S(2)}, u32[]{:S(2)}) %collective-permute-start.1) | collective-permute-done | bytes 53280 | tf_op jit(solution)/shard_map/ppermute | solution.py:200
  12.4 2.0 %collective-permute-start.2 = (bf16[4,104,128]{2,1,0:T(8,128)(2,1)S(1)}, bf16[4,104,128]{2,1,0:T(8,128)(2,1)S(1)}, u32[]{:S(2)}, u32[]{:S(2)}) collective-permute-start(bf16[4,104,128]{2,1,0:T(8,128)(2,1)S(1)} %pad_maximum_fusion.1), channel_id=1, source_target_pairs={{0,8},{1,9},{2,10},{3,11},{4,12},{5,13},{6,14},{7,15},{8,0},{9,1},... | collective-permute-start | bytes 319496 | tf_op jit(solution)/shard_map/ppermute | solution.py:200
  14.4 2.7 %collective-permute-done.2 = bf16[4,104,128]{2,1,0:T(8,128)(2,1)S(1)} collective-permute-done((bf16[4,104,128]{2,1,0:T(8,128)(2,1)S(1)}, bf16[4,104,128]{2,1,0:T(8,128)(2,1)S(1)}, u32[]{:S(2)}, u32[]{:S(2)}) %collective-permute-start.2) | collective-permute-done | bytes 106528 | tf_op jit(solution)/shard_map/ppermute | solution.py:200
  17.2 2.1 %collective-permute-start.3 = (bf16[8,104,128]{2,1,0:T(8,128)(2,1)S(1)}, bf16[8,104,128]{2,1,0:T(8,128)(2,1)S(1)}, u32[]{:S(2)}, u32[]{:S(2)}) collective-permute-start(bf16[8,104,128]{2,1,0:T(8,128)(2,1)S(1)} %pad_maximum_fusion), channel_id=1, source_target_pairs={{0,16},{1,17},{2,18},{3,19},{4,20},{5,21},{6,22},{7,23},{8,24},{9,... | collective-permute-start | bytes 638984 | tf_op jit(solution)/shard_map/ppermute | solution.py:200
  19.3 3.8 %collective-permute-done.3 = bf16[8,104,128]{2,1,0:T(8,128)(2,1)S(1)} collective-permute-done((bf16[8,104,128]{2,1,0:T(8,128)(2,1)S(1)}, bf16[8,104,128]{2,1,0:T(8,128)(2,1)S(1)}, u32[]{:S(2)}, u32[]{:S(2)}) %collective-permute-start.3) | collective-permute-done | bytes 213024 | tf_op jit(solution)/shard_map/ppermute | solution.py:200
  23.1 0.0 copy-start.1
  23.1 0.0 collective-permute-done.4.other_ref
  23.1 2.7 %sums.1 = (f32[40,192]{1,0:T(8,128)S(1)}, f32[40,192]{1,0:T(8,128)S(1)}) custom-call(bf16[16,104,128]{2,1,0:T(8,128)(2,1)S(1)} %constant_dynamic-update-slice_fusion.packed_ref, bf16[32,192]{1,0:T(8,128)(2,1)} %own_ref.1, bf16[32,192]{1,0:T(8,128)(2,1)S(1)} %collective-permute-done.4.other_ref), custom_call_target="tpu_custom_call" | custom-call | flops 1073741824 | bytes 16777216 | tf_op jit(solution)/shard_map/sums/pallas_call | solution.py:215
  25.8 0.1 collective-permute-start.5
  25.9 1.2 %collective-permute-done.5.got_ref = f32[40,192]{1,0:T(8,128)S(1)} collective-permute-done((f32[40,192]{1,0:T(8,128)S(1)}, f32[40,192]{1,0:T(8,128)S(1)}, u32[]{:S(2)}, u32[]{:S(2)}) %collective-permute-start.5) | collective-permute-done | bytes 30752 | tf_op jit(solution)/shard_map/ppermute | solution.py:200
  27.1 0.0 copy-done.1
  27.1 0.2 gram.1
  27.3 0.2 collective-permute-start.6
  27.6 1.0 %collective-permute-done.6 = f32[24,128]{1,0:T(8,128)S(1)} collective-permute-done((f32[24,128]{1,0:T(8,128)S(1)}, f32[24,128]{1,0:T(8,128)S(1)}, u32[]{:S(2)}, u32[]{:S(2)}) %collective-permute-start.6) | collective-permute-done | bytes 12320 | tf_op jit(solution)/shard_map/ppermute | solution.py:200
  28.6 2.0 %collective-permute-start.7 = (f32[24,128]{1,0:T(8,128)S(1)}, f32[24,128]{1,0:T(8,128)S(1)}, u32[]{:S(2)}, u32[]{:S(2)}) collective-permute-start(f32[24,128]{1,0:T(8,128)S(1)} %add.15), channel_id=1, source_target_pairs={{0,8},{1,9},{2,10},{3,11},{4,12},{5,13},{6,14},{7,15},{8,0},{9,1},... | collective-permute-start | bytes 36872 | tf_op jit(solution)/shard_map/ppermute | solution.py:200
  30.6 1.7 %collective-permute-done.7 = f32[24,128]{1,0:T(8,128)S(1)} collective-permute-done((f32[24,128]{1,0:T(8,128)S(1)}, f32[24,128]{1,0:T(8,128)S(1)}, u32[]{:S(2)}, u32[]{:S(2)}) %collective-permute-start.7) | collective-permute-done | bytes 12320 | tf_op jit(solution)/shard_map/ppermute | solution.py:200
  32.3 2.0 %collective-permute-start.8 = (f32[24,128]{1,0:T(8,128)S(1)}, f32[24,128]{1,0:T(8,128)S(1)}, u32[]{:S(2)}, u32[]{:S(2)}) collective-permute-start(f32[24,128]{1,0:T(8,128)S(1)} %add.16), channel_id=1, source_target_pairs={{0,16},{1,17},{2,18},{3,19},{4,20},{5,21},{6,22},{7,23},{8,24},{9,... | collective-permute-start | bytes 36872 | tf_op jit(solution)/shard_map/ppermute | solution.py:200
  34.3 1.7 %collective-permute-done.8 = f32[24,128]{1,0:T(8,128)S(1)} collective-permute-done((f32[24,128]{1,0:T(8,128)S(1)}, f32[24,128]{1,0:T(8,128)S(1)}, u32[]{:S(2)}, u32[]{:S(2)}) %collective-permute-start.8) | collective-permute-done | bytes 12320 | tf_op jit(solution)/shard_map/ppermute | solution.py:200
  36.0 1.9 %collective-permute-start.9 = (f32[24,128]{1,0:T(8,128)S(1)}, f32[24,128]{1,0:T(8,128)S(1)}, u32[]{:S(2)}, u32[]{:S(2)}) collective-permute-start(f32[24,128]{1,0:T(8,128)S(1)} %add.17), channel_id=1, source_target_pairs={{0,1},{1,0},{2,3},{3,2},{4,5},{5,4},{6,7},{7,6},{8,9},{9,8},{10,11... | collective-permute-start | bytes 36872 | tf_op jit(solution)/shard_map/ppermute | solution.py:200
  37.9 1.8 %collective-permute-done.9 = f32[24,128]{1,0:T(8,128)S(1)} collective-permute-done((f32[24,128]{1,0:T(8,128)S(1)}, f32[24,128]{1,0:T(8,128)S(1)}, u32[]{:S(2)}, u32[]{:S(2)}) %collective-permute-start.9) | collective-permute-done | bytes 12320 | tf_op jit(solution)/shard_map/ppermute | solution.py:200
  39.7 2.9 %collective-permute-start.10 = (f32[24,128]{1,0:T(8,128)S(1)}, f32[24,128]{1,0:T(8,128)S(1)}, u32[]{:S(2)}, u32[]{:S(2)}) collective-permute-start(f32[24,128]{1,0:T(8,128)S(1)} %add.18), channel_id=1, source_target_pairs={{0,2},{1,3},{2,0},{3,1},{4,6},{5,7},{6,4},{7,5},{8,10},{9,11},{10,... | collective-permute-start | bytes 36872 | tf_op jit(solution)/shard_map/ppermute | solution.py:200
  42.6 1.7 %collective-permute-done.10 = f32[24,128]{1,0:T(8,128)S(1)} collective-permute-done((f32[24,128]{1,0:T(8,128)S(1)}, f32[24,128]{1,0:T(8,128)S(1)}, u32[]{:S(2)}, u32[]{:S(2)}) %collective-permute-start.10) | collective-permute-done | bytes 12320 | tf_op jit(solution)/shard_map/ppermute | solution.py:200
  44.3 3.6 %whiten.1 = f32[32,192]{1,0:T(8,128)} custom-call(f32[24,128]{1,0:T(8,128)S(1)} %add.19.gram_ref, f32[32,192]{1,0:T(8,128)S(1)} %get-tuple-element.12.diffused_ref, f32[32,192]{1,0:T(8,128)S(1)} %copy-done.1), custom_call_target="tpu_custom_call" | custom-call | flops 1048576 | bytes 16384 | tf_op jit(solution)/shard_map/whiten/pallas_call | solution.py:228
  (13 shorter events, 0.1 us)
Async XLA Ops:
  0.0 0.7 %copy-start.2 = (f32[192]{0:T(256)S(1)}, f32[192]{0:T(256)}, u32[]{:S(2)}) copy-start(f32[192]{0:T(256)} %param.4) | copy-start | bytes 2308
  0.7 0.8 %copy-start = (f32[32,192]{1,0:T(8,128)S(1)}, f32[32,192]{1,0:T(8,128)}, u32[]{:S(2)}) copy-start(f32[32,192]{1,0:T(8,128)} %vec_ref.5) | copy-start | bytes 73732
  2.2 5.9 %collective-permute-start = (bf16[1,104,128]{2,1,0:T(8,128)(2,1)S(1)}, bf16[1,104,128]{2,1,0:T(8,128)(2,1)S(1)}, u32[]{:S(2)}, u32[]{:S(2)}) collective-permute-start(bf16[1,104,128]{2,1,0:T(8,128)(2,1)S(1)} %bitcast.3), channel_id=1, source_target_pairs={{0,2},{1,3},{2,0},{3,1},{4,6},{5,7},{6,4},{7,5},{8,10},{9,11},{10,... | collective-permute-start | bytes 79880 | tf_op jit(solution)/shard_map/ppermute | solution.py:200
  6.3 16.8 %collective-permute-start.4 = (bf16[32,192]{1,0:T(8,128)(2,1)}, bf16[32,192]{1,0:T(8,128)(2,1)S(1)}, u32[]{:S(2)}, u32[]{:S(2)}) collective-permute-start(bf16[32,192]{1,0:T(8,128)(2,1)} %own_ref.1), channel_id=1, source_target_pairs={{0,4},{1,5},{2,6},{3,7},{4,0},{5,1},{6,2},{7,3},{8,12},{9,13},{10,... | collective-permute-start | bytes 36872 | tf_op jit(solution)/shard_map/ppermute | solution.py:200
  8.2 4.2 %collective-permute-start.1 = (bf16[2,104,128]{2,1,0:T(8,128)(2,1)S(1)}, bf16[2,104,128]{2,1,0:T(8,128)(2,1)S(1)}, u32[]{:S(2)}, u32[]{:S(2)}) collective-permute-start(bf16[2,104,128]{2,1,0:T(8,128)(2,1)S(1)} %pad_maximum_fusion.2), channel_id=1, source_target_pairs={{0,1},{1,0},{2,3},{3,2},{4,5},{5,4},{6,7},{7,6},{8,9},{9,8},{10,11... | collective-permute-start | bytes 159752 | tf_op jit(solution)/shard_map/ppermute | solution.py:200
  12.4 4.8 %collective-permute-start.2 = (bf16[4,104,128]{2,1,0:T(8,128)(2,1)S(1)}, bf16[4,104,128]{2,1,0:T(8,128)(2,1)S(1)}, u32[]{:S(2)}, u32[]{:S(2)}) collective-permute-start(bf16[4,104,128]{2,1,0:T(8,128)(2,1)S(1)} %pad_maximum_fusion.1), channel_id=1, source_target_pairs={{0,8},{1,9},{2,10},{3,11},{4,12},{5,13},{6,14},{7,15},{8,0},{9,1},... | collective-permute-start | bytes 319496 | tf_op jit(solution)/shard_map/ppermute | solution.py:200
  17.2 5.9 %collective-permute-start.3 = (bf16[8,104,128]{2,1,0:T(8,128)(2,1)S(1)}, bf16[8,104,128]{2,1,0:T(8,128)(2,1)S(1)}, u32[]{:S(2)}, u32[]{:S(2)}) collective-permute-start(bf16[8,104,128]{2,1,0:T(8,128)(2,1)S(1)} %pad_maximum_fusion), channel_id=1, source_target_pairs={{0,16},{1,17},{2,18},{3,19},{4,20},{5,21},{6,22},{7,23},{8,24},{9,... | collective-permute-start | bytes 638984 | tf_op jit(solution)/shard_map/ppermute | solution.py:200
  23.1 4.0 %copy-start.1 = (f32[32,192]{1,0:T(8,128)S(1)}, f32[32,192]{1,0:T(8,128)}, u32[]{:S(2)}) copy-start(f32[32,192]{1,0:T(8,128)} %vec_ref.5) | copy-start | bytes 73732
  25.8 1.3 %collective-permute-start.5 = (f32[40,192]{1,0:T(8,128)S(1)}, f32[40,192]{1,0:T(8,128)S(1)}, u32[]{:S(2)}, u32[]{:S(2)}) collective-permute-start(f32[40,192]{1,0:T(8,128)S(1)} %get-tuple-element.10), channel_id=1, source_target_pairs={{0,4},{1,5},{2,6},{3,7},{4,0},{5,1},{6,2},{7,3},{8,12},{9,13},{10,... | collective-permute-start | bytes 92168 | tf_op jit(solution)/shard_map/ppermute | solution.py:200
  27.3 1.2 %collective-permute-start.6 = (f32[24,128]{1,0:T(8,128)S(1)}, f32[24,128]{1,0:T(8,128)S(1)}, u32[]{:S(2)}, u32[]{:S(2)}) collective-permute-start(f32[24,128]{1,0:T(8,128)S(1)} %get-tuple-element.11), channel_id=1, source_target_pairs={{0,4},{1,5},{2,6},{3,7},{4,0},{5,1},{6,2},{7,3},{8,12},{9,13},{10,... | collective-permute-start | bytes 36872 | tf_op jit(solution)/shard_map/ppermute | solution.py:200
  28.6 3.7 %collective-permute-start.7 = (f32[24,128]{1,0:T(8,128)S(1)}, f32[24,128]{1,0:T(8,128)S(1)}, u32[]{:S(2)}, u32[]{:S(2)}) collective-permute-start(f32[24,128]{1,0:T(8,128)S(1)} %add.15), channel_id=1, source_target_pairs={{0,8},{1,9},{2,10},{3,11},{4,12},{5,13},{6,14},{7,15},{8,0},{9,1},... | collective-permute-start | bytes 36872 | tf_op jit(solution)/shard_map/ppermute | solution.py:200
  32.3 3.7 %collective-permute-start.8 = (f32[24,128]{1,0:T(8,128)S(1)}, f32[24,128]{1,0:T(8,128)S(1)}, u32[]{:S(2)}, u32[]{:S(2)}) collective-permute-start(f32[24,128]{1,0:T(8,128)S(1)} %add.16), channel_id=1, source_target_pairs={{0,16},{1,17},{2,18},{3,19},{4,20},{5,21},{6,22},{7,23},{8,24},{9,... | collective-permute-start | bytes 36872 | tf_op jit(solution)/shard_map/ppermute | solution.py:200
  36.0 3.7 %collective-permute-start.9 = (f32[24,128]{1,0:T(8,128)S(1)}, f32[24,128]{1,0:T(8,128)S(1)}, u32[]{:S(2)}, u32[]{:S(2)}) collective-permute-start(f32[24,128]{1,0:T(8,128)S(1)} %add.17), channel_id=1, source_target_pairs={{0,1},{1,0},{2,3},{3,2},{4,5},{5,4},{6,7},{7,6},{8,9},{9,8},{10,11... | collective-permute-start | bytes 36872 | tf_op jit(solution)/shard_map/ppermute | solution.py:200
  39.7 4.6 %collective-permute-start.10 = (f32[24,128]{1,0:T(8,128)S(1)}, f32[24,128]{1,0:T(8,128)S(1)}, u32[]{:S(2)}, u32[]{:S(2)}) collective-permute-start(f32[24,128]{1,0:T(8,128)S(1)} %add.18), channel_id=1, source_target_pairs={{0,2},{1,3},{2,0},{3,1},{4,6},{5,7},{6,4},{7,5},{8,10},{9,11},{10,... | collective-permute-start | bytes 36872 | tf_op jit(solution)/shard_map/ppermute | solution.py:200
